TPU v7x, 128 devices: a whole 4x4x4 slice. The times are simulated.
128 devices in a mesh: corpus: 16 (over z, y), fsdp: 2 (over core), tensor: 4 (over x).
Axes of the slice: x: 4, y: 4, z: 4, core: 2. Of those that a mesh axis runs over, the one named last changes fastest.
Arguments:
- queries_in: bfloat16 [4096, 4096], P(('corpus', 'fsdp')), may hold values from -6 to 6
- head_weight: bfloat16 [4096, 4096], P('fsdp', 'tensor'), may hold values from -0.09375 to 0.09375
- passages: bfloat16 [16384, 4096], P('corpus', 'tensor'), may hold values from -0.15625 to 0.15625
- teacher: float32 [4096, 4, 32], P(('corpus', 'fsdp')), may hold values from -250 to 400
- cand_block: int32 [4096, 4], P(('corpus', 'fsdp')), may hold values from 0 to 127, all different within a row; in each aligned block of 128 rows (0 to 127, 128 to 255, ...) at most 6 rows name the same one
- cand_offset: int32 [4096, 4, 32], P(('corpus', 'fsdp')), may hold values from 0 to 127, as said below
- block_slot: int32 [128], replicated, may hold values from 0 to 127, each once
Outputs:
- kl_loss: float32 [4096], P(('corpus', 'fsdp'))
- head_grad: float32 [4096, 4096], P('fsdp', 'tensor')
Inputs may be any that keep to these rules, and one draw needn't show every extreme that they name: `cand_block`: in the rows of one device no block id appears more than 6 times, and some block id appears exactly 6 times there; the 4 ids of one query differ. `cand_offset`: the 32 offsets of one query in one block differ. `block_slot`: each storage position is taken by exactly one block.
All inputs are finite; a program needn't handle non-finite values.
Results may differ from a plain program's by a relative error of at most 0.012.
The roundings to bfloat16 on the way count: a program that leaves them out, or rounds other values in their place, can miss the bound.
Values may be sent and summed in bfloat16 or wider, within the bound.
A program may use at most 128 MiB of HBM per device.

v0:
```python
import jax
import jax.numpy as jnp
from jax import lax
from jax.sharding import PartitionSpec as P

ROWS = 128
MOSTB = 6
SWAP = [(0, 1), (1, 0)]


def on_device(queries_in, head_weight, passages, teacher, cand_block, cand_offset, block_slot):
    query_rows, width = queries_in.shape
    half = width // 2
    cols = head_weight.shape[1]
    per_query = cand_block.shape[1]
    offset_count = cand_offset.shape[2]
    total_blocks = block_slot.shape[0]
    n_corpus = lax.axis_size("corpus")
    blocks_here = passages.shape[0] // ROWS
    slot_total = total_blocks * MOSTB
    slots_each = blocks_here * MOSTB
    picks = query_rows * per_query
    first = lax.axis_index("fsdp") == 0
    low, high = (queries_in[:, :half], queries_in[:, half:])
    mine = jnp.where(first, low, high)
    other = jnp.where(first, high, low)
    theirs = lax.ppermute(other, "fsdp", SWAP)
    part_theirs = jnp.dot(theirs, head_weight, preferred_element_type=jnp.float32)
    back = lax.ppermute(part_theirs, "fsdp", SWAP)
    part_mine = jnp.dot(mine, head_weight, preferred_element_type=jnp.float32)
    query = (part_mine + back).astype(jnp.bfloat16)
    all_mine = lax.all_gather(mine, "corpus", axis=0, tiled=True)
    all_theirs = lax.all_gather(theirs, "corpus", axis=0, tiled=True)
    block_ids = lax.broadcasted_iota(jnp.int32, (1, total_blocks), 1)
    named = (cand_block.reshape(-1, 1) == block_ids).astype(jnp.int32)
    slot_of = jnp.sum(named * block_slot.reshape(1, -1), axis=1)
    hits = slot_of[:, None] == block_ids
    before = (
        lax.broadcasted_iota(jnp.int32, (picks, picks), 1)
        < lax.broadcasted_iota(jnp.int32, (picks, picks), 0)
    ).astype(jnp.bfloat16)
    earlier = jnp.dot(before, hits.astype(jnp.bfloat16), preferred_element_type=jnp.float32)
    slot_rank = jnp.sum(jnp.where(hits, earlier, 0.0), axis=1).astype(jnp.int32)
    position = slot_of * MOSTB + slot_rank
    slot_ids = lax.broadcasted_iota(jnp.int32, (slot_total, 1), 0)
    place = (slot_ids == position.reshape(1, -1)).astype(jnp.bfloat16)
    by_query = position.reshape(query_rows, per_query)
    owner = slot_ids == by_query[:, 0].reshape(1, -1)
    for g in range(1, per_query):
        owner = owner | (slot_ids == by_query[:, g].reshape(1, -1))
    owner = owner.astype(jnp.bfloat16)
    slot_block = slot_ids % slots_each // MOSTB
    send_queries = jnp.dot(owner, query, preferred_element_type=jnp.float32).astype(jnp.bfloat16)
    got_queries = lax.all_to_all(
        send_queries.reshape(n_corpus, slots_each, cols), "corpus", 0, 0, tiled=True
    ).reshape(slot_total, cols)
    wide = lax.dot_general(
        got_queries, passages, (((1,), (1,)), ((), ())), preferred_element_type=jnp.float32
    )
    scores = wide[:, :ROWS]
    for j in range(1, blocks_here):
        scores = jnp.where(slot_block == j, wide[:, j * ROWS : (j + 1) * ROWS], scores)
    returned = lax.all_to_all(
        scores.reshape(n_corpus, slots_each, ROWS), "corpus", 0, 0, tiled=True
    ).reshape(slot_total, ROWS)
    picked = returned[position]
    offsets = cand_offset.reshape(picks, offset_count)
    row_ids = lax.broadcasted_iota(jnp.int32, (1, 1, ROWS), 2)
    chosen = offsets[:, :, None] == row_ids
    partial = jnp.sum(jnp.where(chosen, picked[:, None, :], 0.0), axis=2)
    total = partial.reshape(query_rows, per_query * offset_count)
    total = total + lax.ppermute(total, "tensor", [(0, 1), (1, 0), (2, 3), (3, 2)])
    total = total + lax.ppermute(total, "tensor", [(0, 2), (2, 0), (1, 3), (3, 1)])
    student = 50.0 * total
    cached = teacher.reshape(query_rows, per_query * offset_count)
    log_student = student - jax.nn.logsumexp(student, axis=1, keepdims=True)
    log_teacher = cached - jax.nn.logsumexp(cached, axis=1, keepdims=True)
    prob_teacher = jnp.exp(log_teacher)
    kl_loss = jnp.sum(prob_teacher * (log_teacher - log_student), axis=1)
    dscore = (50.0 * (jnp.exp(log_student) - prob_teacher)).astype(jnp.bfloat16)
    spread = jnp.sum(
        jnp.where(chosen, dscore.reshape(picks, offset_count, 1).astype(jnp.float32), 0.0), axis=1
    ).astype(jnp.bfloat16)
    dense = jnp.dot(place, spread, preferred_element_type=jnp.float32).astype(jnp.bfloat16)
    got_dense = lax.all_to_all(
        dense.reshape(n_corpus, slots_each, ROWS), "corpus", 0, 0, tiled=True
    ).reshape(slot_total, ROWS)
    expanded = jnp.concatenate(
        [jnp.where(slot_block == j, got_dense, jnp.bfloat16(0)) for j in range(blocks_here)], axis=1
    )
    block_part = jnp.dot(expanded, passages, preferred_element_type=jnp.float32).astype(
        jnp.bfloat16
    )
    arrived = lax.all_to_all(
        block_part.reshape(n_corpus, slots_each, cols), "corpus", 0, 0, tiled=True
    ).reshape(slot_total, cols)
    query_grad = lax.dot_general(
        owner, arrived, (((0,), (0,)), ((), ())), preferred_element_type=jnp.float32
    ).astype(jnp.bfloat16)
    grad_mine = lax.all_gather(query_grad, "corpus", axis=0, tiled=True)
    grad_theirs = lax.ppermute(grad_mine, "fsdp", SWAP)
    across = (((0,), (0,)), ((), ()))
    head_grad = lax.dot_general(
        all_mine, grad_mine, across, preferred_element_type=jnp.float32
    ) + lax.dot_general(all_theirs, grad_theirs, across, preferred_element_type=jnp.float32)
    return (kl_loss, head_grad)


def solution(mesh):
    placed = (
        P(("corpus", "fsdp"), None),
        P("fsdp", "tensor"),
        P("corpus", "tensor"),
        P(("corpus", "fsdp"), None, None),
        P(("corpus", "fsdp"), None),
        P(("corpus", "fsdp"), None, None),
        P(),
    )
    return jax.shard_map(
        on_device,
        mesh=mesh,
        in_specs=placed,
        out_specs=(P(("corpus", "fsdp")), P("fsdp", "tensor")),
        check_vma=False,
    )
```

profile of v0, /device:TPU:1, one launch (start us, length us, event | category | flops | bytes accessed | tf_op | source)
XLA Modules:
  0.0 353.7 jit_solution(15698942265412292982)
XLA Ops:
  7.2 2.2 broadcast_select_fusion
  11.0 1.5 collective-permute-done
  12.5 3.9 %fusion.26 = f32[128,1024]{1,0:T(8,128)} fusion(bf16[128,2048]{1,0:T(8,128)(2,1)S(1)} %collective-permute-done, bf16[2048,1024]{1,0:T(8,128)(2,1)} %param.8), kind=kOutput, calls=%fused_computation.91 | convolution fusion | flops 536870912 | bytes 5242880 | tf_op jit(solution)/shard_map/dot_general | solution.py:28
  18.7 4.6 %convolution_convert_fusion = bf16[768,1024]{1,0:T(8,128)(2,1)} fusion(f32[128,1024]{1,0:T(8,128)} %collective-permute-done.1, s32[128]{0:T(128)S(1)} %get-tuple-element.3, s32[128]{0:T(128)S(1)} %get-tuple-element.4, s32[128]{0:T(128)S(1)} %get-tuple-element.5, s32[128]{0:T(128)S(1)} %get-tuple-element.2, bf16[128,2048]{1,0:T(8,128)(2,1)S(1)} %get-tuple-element.9, ...), kind=kOutput, calls=%fused_computation.5 | convolution fusion | flops 739934208 | bytes 6817792 | tf_op jit(solution)/shard_map/dot_general | solution.py:53
  23.3 7.9 %all-to-all-start = ((bf16[16,48,1024]{2,1,0:T(8,128)(2,1)}), bf16[16,48,1024]{2,1,0:T(8,128)(2,1)}, u32[]{:S(2)}, u32[]{:S(2)}) async-start(bf16[16,48,1024]{2,1,0:T(8,128)(2,1)} %bitcast.46), calls=%async_computation | async-start | bytes 3145728 | tf_op jit(solution)/shard_map/all_to_all | solution.py:54
  31.4 23.9 %all-to-all-done = bf16[16,48,1024]{2,1,0:T(8,128)(2,1)} async-done(((bf16[16,48,1024]{2,1,0:T(8,128)(2,1)}), bf16[16,48,1024]{2,1,0:T(8,128)(2,1)}, u32[]{:S(2)}, u32[]{:S(2)}) %all-to-all-start) | async-done | bytes 1572896 | tf_op jit(solution)/shard_map/all_to_all | solution.py:54
  55.3 3.2 fusion.27
  58.6 2.1 fusion.9
  60.7 4.1 %all-to-all-start.1 = ((f32[16,48,128]{2,1,0:T(8,128)}), f32[16,48,128]{2,1,0:T(8,128)S(1)}, u32[]{:S(2)}, u32[]{:S(2)}) async-start(f32[16,48,128]{2,1,0:T(8,128)} %bitcast.4), calls=%async_computation.1 | async-start | bytes 786432 | tf_op jit(solution)/shard_map/all_to_all | solution.py:63
  65.0 8.7 %all-to-all-done.1 = f32[16,48,128]{2,1,0:T(8,128)S(1)} async-done(((f32[16,48,128]{2,1,0:T(8,128)}), f32[16,48,128]{2,1,0:T(8,128)S(1)}, u32[]{:S(2)}, u32[]{:S(2)}) %all-to-all-start.1) | async-done | bytes 393248 | tf_op jit(solution)/shard_map/all_to_all | solution.py:63
  74.8 5.1 %select_reduce_fusion.1 = f32[512,32]{1,0:T(8,128)S(1)} fusion(f32[512,128]{1,0:T(8,128)S(1)} %gather_fusion, s32[512,32]{1,0:T(8,128)S(1)} %bitcast.47), kind=kLoop, calls=%fused_computation.2 | loop fusion | flops 6275072 | bytes 393216 | tf_op jit(solution)/shard_map/reduce_sum | solution.py:70
  81.5 1.9 collective-permute-done.2
  83.3 2.8 collective-permute-start.3
  86.2 2.6 collective-permute-done.3
  89.6 5.6 %select_reduce_fusion = bf16[512,128]{1,0:T(8,128)(2,1)S(1)} fusion(f32[512,32]{1,0:T(8,128)S(1)} %reshape.201, s32[512,32]{1,0:T(8,128)S(1)} %bitcast.48), kind=kLoop, calls=%fused_computation.1 | loop fusion | flops 6225920 | bytes 262144 | tf_op jit(solution)/shard_map/reduce_sum | solution.py:81
  96.3 3.5 all-to-all-start.2
  99.9 7.1 %all-to-all-done.2 = bf16[16,48,128]{2,1,0:T(8,128)(2,1)S(1)} async-done(((bf16[16,48,128]{2,1,0:T(8,128)(2,1)}), bf16[16,48,128]{2,1,0:T(8,128)(2,1)S(1)}, u32[]{:S(2)}, u32[]{:S(2)}) %all-to-all-start.2) | async-done | bytes 196640 | tf_op jit(solution)/shard_map/all_to_all | solution.py:85
  108.7 1.8 convolution_convert_fusion.1
  110.5 21.1 %all_to_all.20 = bf16[16,48,1024]{2,1,0:T(8,128)(2,1)S(1)} all-to-all(bf16[16,48,1024]{2,1,0:T(8,128)(2,1)S(1)} %bitcast.50), channel_id=1, replica_groups=mesh['corpus'=16,'fsdp'=2,'tensor'=4] {'corpus'}, dimensions={0} | all-to-all | bytes 3145728 | tf_op jit(solution)/shard_map/all_to_all | solution.py:94
  134.3 51.5 %all-gather.6.cloned.1.call-done = bf16[2048,1024]{1,0:T(8,128)(2,1)} async-done(((bf16[128,1024]{1,0:T(8,128)(2,1)}), bf16[2048,1024]{1,0:T(8,128)(2,1)}) %all-gather.6.cloned.1.call-update) | async-done | bytes 4194320 | tf_op jit(solution)/shard_map/all_gather | solution.py:100
  186.6 71.8 %all-gather.4.cloned.1.call-done = bf16[2048,2048]{1,0:T(8,128)(2,1)} async-done(((bf16[128,2048]{1,0:T(8,128)(2,1)}), bf16[2048,2048]{1,0:T(8,128)(2,1)}) %all-gather.4.cloned.1.call-update) | async-done | bytes 8388624 | tf_op jit(solution)/shard_map/all_gather | solution.py:32
  258.5 14.6 %fusion.28 = f32[2048,1024]{1,0:T(8,128)} fusion(bf16[2048,2048]{1,0:T(8,128)(2,1)} %all-gather.4.cloned.1.call-done, bf16[2048,1024]{1,0:T(8,128)(2,1)} %all-gather.6.cloned.1.call-done), kind=kOutput, calls=%fused_computation.93 | convolution fusion | flops 8589934592 | bytes 20971520 | tf_op jit(solution)/shard_map/dot_general | solution.py:103
  273.1 58.1 %all-gather.8.cloned.1.call-done = bf16[2048,2048]{1,0:T(8,128)(2,1)} async-done(((bf16[128,2048]{1,0:T(8,128)(2,1)}), bf16[2048,2048]{1,0:T(8,128)(2,1)}) %all-gather.8.cloned.1.call-update) | async-done | bytes 8388624 | tf_op jit(solution)/shard_map/all_gather | solution.py:33
  331.2 16.0 %convolution_add_fusion = f32[2048,1024]{1,0:T(8,128)} fusion(f32[2048,1024]{1,0:T(8,128)} %fusion.28, bf16[2048,2048]{1,0:T(8,128)(2,1)} %all-gather.8.cloned.1.call-done, bf16[2048,1024]{1,0:T(8,128)(2,1)} %collective-permute-done.4), kind=kOutput, calls=%fused_computation.4 | convolution fusion | flops 8592031744 | bytes 29360128 | tf_op jit(solution)/shard_map/dot_general | solution.py:105
  (69 shorter events, 13.8 us)
Async XLA Ops:
  7.2 48.1 %copy-start = (bf16[1024,1024]{1,0:T(8,128)(2,1)S(1)}, bf16[1024,1024]{1,0:T(8,128)(2,1)}, u32[]{:S(2)}) copy-start(bf16[1024,1024]{1,0:T(8,128)(2,1)} %param.9) | copy-start | bytes 6291460
  7.2 3.6 %copy-start.6 = (s32[128,4]{0,1:T(4,128)S(1)}, s32[128,4]{0,1:T(4,128)}, u32[]{:S(2)}) copy-start(s32[128,4]{0,1:T(4,128)} %param.11) | copy-start | bytes 6148
  9.4 9.3 %copy-start.2 = (bf16[128,2048]{1,0:T(8,128)(2,1)}, bf16[128,2048]{1,0:T(8,128)(2,1)S(1)}, u32[]{:S(2)}) copy-start(bf16[128,2048]{1,0:T(8,128)(2,1)S(1)} %get-tuple-element.9) | copy-start | bytes 1572868
  9.4 3.1 collective-permute-start
  12.5 3.9 %copy-start.3 = (bf16[128,2048]{1,0:T(8,128)(2,1)}, bf16[128,2048]{1,0:T(8,128)(2,1)S(1)}, u32[]{:S(2)}) copy-start(bf16[128,2048]{1,0:T(8,128)(2,1)S(1)} %collective-permute-done) | copy-start | bytes 1572868
  12.5 4.3 %copy-start.7 = (s32[128]{0:T(128)S(1)}, s32[128]{0:T(128)}, u32[]{:S(2)}) copy-start(s32[128]{0:T(128)} %param.13) | copy-start | bytes 1540
  16.5 2.3 collective-permute-start.1
  23.3 32.0 %all-to-all-start = ((bf16[16,48,1024]{2,1,0:T(8,128)(2,1)}), bf16[16,48,1024]{2,1,0:T(8,128)(2,1)}, u32[]{:S(2)}, u32[]{:S(2)}) async-start(bf16[16,48,1024]{2,1,0:T(8,128)(2,1)} %bitcast.46), calls=%async_computation | async-start | bytes 3145728 | tf_op jit(solution)/shard_map/all_to_all | solution.py:54
  58.5 6.2 %copy-start.5 = (s32[128,4,32]{0,2,1:T(8,128)S(1)}, s32[128,4,32]{0,2,1:T(8,128)}, u32[]{:S(2)}) copy-start(s32[128,4,32]{0,2,1:T(8,128)} %param.12) | copy-start | bytes 196612
  58.6 6.4 %copy-start.4 = (f32[128,4,32]{0,2,1:T(8,128)S(1)}, f32[128,4,32]{0,2,1:T(8,128)}, u32[]{:S(2)}) copy-start(f32[128,4,32]{0,2,1:T(8,128)} %param.10) | copy-start | bytes 196612
  60.7 13.1 %all-to-all-start.1 = ((f32[16,48,128]{2,1,0:T(8,128)}), f32[16,48,128]{2,1,0:T(8,128)S(1)}, u32[]{:S(2)}, u32[]{:S(2)}) async-start(f32[16,48,128]{2,1,0:T(8,128)} %bitcast.4), calls=%async_computation.1 | async-start | bytes 786432 | tf_op jit(solution)/shard_map/all_to_all | solution.py:63
  80.1 3.2 collective-permute-start.2
  83.3 5.4 %collective-permute-start.3 = (f32[128,128]{0,1:T(8,128)S(1)}, f32[128,128]{0,1:T(8,128)S(1)}, u32[]{:S(2)}, u32[]{:S(2)}) collective-permute-start(f32[128,128]{0,1:T(8,128)S(1)} %add.157), channel_id=1, source_target_pairs={{0,2},{2,0},{1,3},{3,1},{4,6},{6,4},{5,7},{7,5},{8,10},{10,8},{9,1... | collective-permute-start | bytes 196616 | tf_op jit(solution)/shard_map/ppermute | solution.py:73
  96.3 10.7 %all-to-all-start.2 = ((bf16[16,48,128]{2,1,0:T(8,128)(2,1)}), bf16[16,48,128]{2,1,0:T(8,128)(2,1)S(1)}, u32[]{:S(2)}, u32[]{:S(2)}) async-start(bf16[16,48,128]{2,1,0:T(8,128)(2,1)} %bitcast.8), calls=%async_computation.2 | async-start | bytes 393216 | tf_op jit(solution)/shard_map/all_to_all | solution.py:85
  99.8 85.9 %all-gather.6.cloned.1.call-start = ((), (), s32[]{:S(2)}) async-start(), calls=%async_computation.5 | async-start | bytes 4456448 | tf_op jit(solution)/shard_map/all_gather | solution.py:100
  132.8 125.6 %all-gather.4.cloned.1.call-start = ((), (), s32[]{:S(2)}) async-start(), calls=%async_computation.4 | async-start | bytes 8912896 | tf_op jit(solution)/shard_map/all_gather | solution.py:32
  133.6 197.6 %all-gather.8.cloned.1.call-start = ((), (), s32[]{:S(2)}) async-start(), calls=%async_computation.6 | async-start | bytes 8912896 | tf_op jit(solution)/shard_map/all_gather | solution.py:33
  185.8 145.4 %collective-permute-start.4 = (bf16[2048,1024]{1,0:T(8,128)(2,1)}, bf16[2048,1024]{1,0:T(8,128)(2,1)}, u32[]{:S(2)}, u32[]{:S(2)}) collective-permute-start(bf16[2048,1024]{1,0:T(8,128)(2,1)} %all-gather.6.cloned.1.call-done), channel_id=1, source_target_pairs={{0,4},{4,0},{1,5},{5,1},{2,6},{6,2},{3,7},{7,3},{8,12},{12,8},{9,1... | collective-permute-start | bytes 12582920 | tf_op jit(solution)/shard_map/ppermute | solution.py:101
  331.2 16.0 %copy-start.1 = (bf16[1024,1024]{1,0:T(8,128)(2,1)S(1)}, bf16[1024,1024]{1,0:T(8,128)(2,1)}, u32[]{:S(2)}) copy-start(bf16[1024,1024]{1,0:T(8,128)(2,1)} %param.9) | copy-start | bytes 6291460
Sparse Core Ops, SparseCore 0:
  132.9 52.7 all-gather.5
  187.9 70.5 all-gather.3
  260.6 70.5 all-gather.7
where the time goes:
time: 354 us
  waiting for transfers between devices  229 us (65%)
  matrix products  46.7 us (13%)
  starting transfers between devices  22.4 us (6%)
  blocking collectives  21.1 us (6%)
  other arithmetic  17.3 us (5%)
  between operations  14 us (4%)
    all_gather x1, waiting for transfers between devices, on_device(): all_mine = lax.all_gather(mine, 'corpus', axis=0, tiled=True)  71.8 us
    all_gather x1, waiting for transfers between devices, on_device(): all_theirs = lax.all_gather(theirs, 'corpus', axis=0, tiled=True)  58.1 us
    all_gather x1, waiting for transfers between devices, on_device(): grad_mine = lax.all_gather(query_grad, 'corpus', axis=0, tiled=True)  51.5 us
    all_to_all x1, waiting for transfers between devices, on_device(): lax.all_to_all(send_queries.reshape(n_corpus, slots_each, cols), 'corpus'...  23.9 us
    all_to_all x1, blocking collectives, on_device(): lax.all_to_all(block_part.reshape(n_corpus, slots_each, cols), 'corpus',...  21.1 us
    dot_general x1, matrix products, on_device(): lax.dot_general(all_theirs, grad_theirs, across, preferred_element_type=j...  16 us
    dot_general x1, matrix products, on_device(): lax.dot_general(all_mine, grad_mine, across, preferred_element_type=jnp.f...  14.6 us
    all_to_all x1, waiting for transfers between devices, on_device(): lax.all_to_all(scores.reshape(n_corpus, slots_each, ROWS), 'corpus', 0, 0...  8.74 us
  transfers between devices with their start and end apart: 11, of which 10 were waited for; matrix products, arithmetic and copies ran while one was open for 5% of the time, Pallas kernels for 0%

commit v1 on v0

--- a/solution.py
+++ b/solution.py
@@ -6,6 +6,12 @@
 ROWS = 128
 MOSTB = 6
 SWAP = [(0, 1), (1, 0)]
+
+
+def joined_along(blocks, dim):
+    dims = list(blocks.shape[1:])
+    dims[dim] *= blocks.shape[0]
+    return jnp.moveaxis(blocks, 0, dim).reshape(dims)
 
 
 def on_device(queries_in, head_weight, passages, teacher, cand_block, cand_offset, block_slot):
@@ -97,7 +103,19 @@
     query_grad = lax.dot_general(
         owner, arrived, (((0,), (0,)), ((), ())), preferred_element_type=jnp.float32
     ).astype(jnp.bfloat16)
-    grad_mine = lax.all_gather(query_grad, "corpus", axis=0, tiled=True)
+    size = lax.axis_size("corpus")
+    pairs = [(i, (i + 1) % size) for i in range(size)]
+    back_2 = [(b, a) for a, b in pairs]
+    lower, upper = ([], [])
+    for step in range(size - 1):
+        if step % 2 == 0:
+            lower.append(lax.ppermute(lower[-1] if lower else query_grad, "corpus", pairs))
+        else:
+            upper.append(lax.ppermute(upper[-1] if upper else query_grad, "corpus", back_2))
+    blocks = jnp.stack([*lower[::-1], query_grad, *upper])
+    shift = lax.axis_index("corpus") - len(lower)
+    blocks = blocks[(jnp.arange(size) - shift) % size]
+    grad_mine = joined_along(blocks, 0)
     grad_theirs = lax.ppermute(grad_mine, "fsdp", SWAP)
     across = (((0,), (0,)), ((), ()))
     head_grad = lax.dot_general(

time: 354 us -> 329 us (0.929)
  waiting for transfers between devices: 229 us -> 122 us
  starting transfers between devices: 22.4 us -> 79.3 us
  local copies, waits for them, and re-layouts: 2.67 us -> 22.5 us
  blocking collectives: 21.1 us -> 27.3 us
    all_gather x1, waiting for transfers between devices: 71.8 us -> 0.01 us  [on_device(): all_mine = lax.all_gather(mine, 'corpus', axis=0, tiled=True)]
    ppermute x0 -> x15, waiting for transfers between devices: none -> 60.1 us  [the longest x8 47.2 us: on_device(): lax.ppermute(lower[-1] if lower else query_grad, 'corpus', pairs)]
    all_gather x1, waiting for transfers between devices: 58.1 us -> 0.01 us  [on_device(): all_theirs = lax.all_gather(theirs, 'corpus', axis=0, tiled=True)]
    all_gather x1 -> x0, waiting for transfers between devices: 51.5 us -> none  [on_device(): grad_mine = lax.all_gather(query_grad, 'corpus', axis=0, tiled=True)]
    ppermute x0 -> x15, starting transfers between devices: none -> 35.9 us  [the longest x7 35.5 us: on_device(): lax.ppermute(upper[-1] if upper else query_grad, 'corpus', back_2)]
    ppermute x1, starting transfers between devices: 0.84 us -> 20.3 us  [on_device(): grad_theirs = lax.ppermute(grad_mine, 'fsdp', SWAP)]
    unnamed x25 -> x38, local copies, waits for them, and re-layouts: 0.73 us -> 14.9 us
    ppermute x1, waiting for transfers between devices: 0.01 us -> 7.13 us  [on_device(): grad_theirs = lax.ppermute(grad_mine, 'fsdp', SWAP)]
  transfers between devices with their start and end apart: 11 -> 25, of which waited for: 10 -> 19; matrix products, arithmetic and copies ran while one was open for 5% -> 20% of each run, Pallas kernels for 0% -> 0%
where the time goes in v1:
time: 329 us; the launch traced here: 328 us
  waiting for transfers between devices  122 us (37%)
  starting transfers between devices  79.3 us (24%)
  matrix products  45.8 us (14%)
  blocking collectives  27.3 us (8%)
  local copies, waits for them, and re-layouts  22.5 us (7%)
  other arithmetic  16.5 us (5%)
  between operations  14.4 us (4%)
    ppermute x8, waiting for transfers between devices, on_device(): lax.ppermute(lower[-1] if lower else query_grad, 'corpus', pairs)  47.2 us
    ppermute x7, starting transfers between devices, on_device(): lax.ppermute(upper[-1] if upper else query_grad, 'corpus', back_2)  35.5 us
    all_to_all x1, blocking collectives, on_device(): lax.all_to_all(block_part.reshape(n_corpus, slots_each, cols), 'corpus',...  27.3 us
    all_to_all x1, waiting for transfers between devices, on_device(): lax.all_to_all(send_queries.reshape(n_corpus, slots_each, cols), 'corpus'...  27.2 us
    ppermute x1, starting transfers between devices, on_device(): grad_theirs = lax.ppermute(grad_mine, 'fsdp', SWAP)  20.3 us
    dot_general x1, matrix products, on_device(): lax.dot_general(all_mine, grad_mine, across, preferred_element_type=jnp.f...  16 us
    unnamed x38, local copies, waits for them, and re-layouts  14.9 us
    dot_general x1, matrix products, on_device(): lax.dot_general(all_theirs, grad_theirs, across, preferred_element_type=j...  14.6 us
  transfers between devices with their start and end apart: 25, of which 19 were waited for; matrix products, arithmetic and copies ran while one was open for 20% of the time, Pallas kernels for 0%

profile of v1, /device:TPU:1, one launch (start us, length us, event | category | flops | bytes accessed | tf_op | source)
XLA Modules:
  0.0 328.2 jit_solution(8228447870690326612)
XLA Ops:
  23.9 7.9 %all-to-all-start = ((bf16[16,48,1024]{2,1,0:T(8,128)(2,1)}), bf16[16,48,1024]{2,1,0:T(8,128)(2,1)}, u32[]{:S(2)}, u32[]{:S(2)}) async-start(bf16[16,48,1024]{2,1,0:T(8,128)(2,1)} %bitcast.81), calls=%async_computation | async-start | bytes 3145728 | tf_op jit(solution)/shard_map/all_to_all | solution.py:60
  31.9 27.2 %all-to-all-done = bf16[16,48,1024]{2,1,0:T(8,128)(2,1)} async-done(((bf16[16,48,1024]{2,1,0:T(8,128)(2,1)}), bf16[16,48,1024]{2,1,0:T(8,128)(2,1)}, u32[]{:S(2)}, u32[]{:S(2)}) %all-to-all-start) | async-done | bytes 1572896 | tf_op jit(solution)/shard_map/all_to_all | solution.py:60
  64.5 5.6 %all-to-all-start.1 = ((f32[16,48,128]{2,1,0:T(8,128)}), f32[16,48,128]{2,1,0:T(8,128)S(1)}, u32[]{:S(2)}, u32[]{:S(2)}) async-start(f32[16,48,128]{2,1,0:T(8,128)} %bitcast.4), calls=%async_computation.1 | async-start | bytes 786432 | tf_op jit(solution)/shard_map/all_to_all | solution.py:69
  70.3 14.0 %all-to-all-done.1 = f32[16,48,128]{2,1,0:T(8,128)S(1)} async-done(((f32[16,48,128]{2,1,0:T(8,128)}), f32[16,48,128]{2,1,0:T(8,128)S(1)}, u32[]{:S(2)}, u32[]{:S(2)}) %all-to-all-start.1) | async-done | bytes 393248 | tf_op jit(solution)/shard_map/all_to_all | solution.py:69
  85.3 5.1 %select_reduce_fusion.1 = f32[512,32]{1,0:T(8,128)S(1)} fusion(f32[512,128]{1,0:T(8,128)S(1)} %gather_fusion, s32[512,32]{1,0:T(8,128)S(1)} %bitcast.84), kind=kLoop, calls=%fused_computation.3 | loop fusion | flops 6275072 | bytes 393216 | tf_op jit(solution)/shard_map/reduce_sum | solution.py:76
  100.2 5.6 %select_reduce_fusion = bf16[512,128]{1,0:T(8,128)(2,1)S(1)} fusion(f32[512,32]{1,0:T(8,128)S(1)} %reshape.254, s32[512,32]{1,0:T(8,128)S(1)} %bitcast.85), kind=kLoop, calls=%fused_computation.2 | loop fusion | flops 6225920 | bytes 262144 | tf_op jit(solution)/shard_map/reduce_sum | solution.py:87
  111.2 6.4 %all-to-all-done.2 = bf16[16,48,128]{2,1,0:T(8,128)(2,1)S(1)} async-done(((bf16[16,48,128]{2,1,0:T(8,128)(2,1)}), bf16[16,48,128]{2,1,0:T(8,128)(2,1)S(1)}, u32[]{:S(2)}, u32[]{:S(2)}) %all-to-all-start.2) | async-done | bytes 196640 | tf_op jit(solution)/shard_map/all_to_all | solution.py:91
  121.2 27.3 %all_to_all.20 = bf16[16,48,1024]{2,1,0:T(8,128)(2,1)S(1)} all-to-all(bf16[16,48,1024]{2,1,0:T(8,128)(2,1)S(1)} %bitcast.87), channel_id=1, replica_groups=mesh['corpus'=16,'fsdp'=2,'tensor'=4] {'corpus'}, dimensions={0} | all-to-all | bytes 3145728 | tf_op jit(solution)/shard_map/all_to_all | solution.py:100
  149.3 8.5 %collective-permute-done.4 = bf16[128,1024]{1,0:T(8,128)(2,1)S(1)} collective-permute-done((bf16[128,1024]{1,0:T(8,128)(2,1)S(1)}, bf16[128,1024]{1,0:T(8,128)(2,1)S(1)}, u32[]{:S(2)}, u32[]{:S(2)}) %collective-permute-start.4) | collective-permute-done | bytes 262176 | tf_op jit(solution)/shard_map/ppermute | solution.py:112
  162.5 5.7 %collective-permute-done.5 = bf16[128,1024]{1,0:T(8,128)(2,1)S(1)} collective-permute-done((bf16[128,1024]{1,0:T(8,128)(2,1)S(1)}, bf16[128,1024]{1,0:T(8,128)(2,1)S(1)}, u32[]{:S(2)}, u32[]{:S(2)}) %collective-permute-start.5) | collective-permute-done | bytes 262176 | tf_op jit(solution)/shard_map/ppermute | solution.py:112
  171.6 5.2 %collective-permute-start.13 = (bf16[128,1024]{1,0:T(8,128)(2,1)S(1)}, bf16[128,1024]{1,0:T(8,128)(2,1)S(1)}, u32[]{:S(2)}, u32[]{:S(2)}) collective-permute-start(bf16[128,1024]{1,0:T(8,128)(2,1)S(1)} %collective-permute-done.12), channel_id=1, source_target_pairs={{8,0},{16,8},{24,16},{32,24},{40,32},{48,40},{56,48},{64,56},{72,6... | collective-permute-start | bytes 786440 | tf_op jit(solution)/shard_map/ppermute | solution.py:114
  176.8 6.4 %collective-permute-done.6 = bf16[128,1024]{1,0:T(8,128)(2,1)S(1)} collective-permute-done((bf16[128,1024]{1,0:T(8,128)(2,1)S(1)}, bf16[128,1024]{1,0:T(8,128)(2,1)S(1)}, u32[]{:S(2)}, u32[]{:S(2)}) %collective-permute-start.6) | collective-permute-done | bytes 262176 | tf_op jit(solution)/shard_map/ppermute | solution.py:112
  187.4 5.5 %collective-permute-start.14 = (bf16[128,1024]{1,0:T(8,128)(2,1)S(1)}, bf16[128,1024]{1,0:T(8,128)(2,1)S(1)}, u32[]{:S(2)}, u32[]{:S(2)}) collective-permute-start(bf16[128,1024]{1,0:T(8,128)(2,1)S(1)} %collective-permute-done.13), channel_id=1, source_target_pairs={{8,0},{16,8},{24,16},{32,24},{40,32},{48,40},{56,48},{64,56},{72,6... | collective-permute-start | bytes 786440 | tf_op jit(solution)/shard_map/ppermute | solution.py:114
  193.0 5.2 %collective-permute-done.7 = bf16[128,1024]{1,0:T(8,128)(2,1)S(1)} collective-permute-done((bf16[128,1024]{1,0:T(8,128)(2,1)S(1)}, bf16[128,1024]{1,0:T(8,128)(2,1)S(1)}, u32[]{:S(2)}, u32[]{:S(2)}) %collective-permute-start.7) | collective-permute-done | bytes 262176 | tf_op jit(solution)/shard_map/ppermute | solution.py:112
  198.2 5.3 %collective-permute-done.14 = bf16[128,1024]{1,0:T(8,128)(2,1)S(1)} collective-permute-done((bf16[128,1024]{1,0:T(8,128)(2,1)S(1)}, bf16[128,1024]{1,0:T(8,128)(2,1)S(1)}, u32[]{:S(2)}, u32[]{:S(2)}) %collective-permute-start.14) | collective-permute-done | bytes 262176 | tf_op jit(solution)/shard_map/ppermute | solution.py:114
  203.4 5.5 %collective-permute-start.15 = (bf16[128,1024]{1,0:T(8,128)(2,1)S(1)}, bf16[128,1024]{1,0:T(8,128)(2,1)S(1)}, u32[]{:S(2)}, u32[]{:S(2)}) collective-permute-start(bf16[128,1024]{1,0:T(8,128)(2,1)S(1)} %collective-permute-done.14), channel_id=1, source_target_pairs={{8,0},{16,8},{24,16},{32,24},{40,32},{48,40},{56,48},{64,56},{72,6... | collective-permute-start | bytes 786440 | tf_op jit(solution)/shard_map/ppermute | solution.py:114
  227.2 5.9 %collective-permute-done.10 = bf16[128,1024]{1,0:T(8,128)(2,1)} collective-permute-done((bf16[128,1024]{1,0:T(8,128)(2,1)S(1)}, bf16[128,1024]{1,0:T(8,128)(2,1)}, u32[]{:S(2)}, u32[]{:S(2)}) %collective-permute-start.10) | collective-permute-done | bytes 262176 | tf_op jit(solution)/shard_map/ppermute | solution.py:112
  233.2 4.9 %collective-permute-start.18 = (bf16[128,1024]{1,0:T(8,128)(2,1)S(1)}, bf16[128,1024]{1,0:T(8,128)(2,1)S(1)}, u32[]{:S(2)}, u32[]{:S(2)}) collective-permute-start(bf16[128,1024]{1,0:T(8,128)(2,1)S(1)} %collective-permute-done.17), channel_id=1, source_target_pairs={{8,0},{16,8},{24,16},{32,24},{40,32},{48,40},{56,48},{64,56},{72,6... | collective-permute-start | bytes 786440 | tf_op jit(solution)/shard_map/ppermute | solution.py:114
  238.1 6.8 %collective-permute-done.11 = bf16[128,1024]{1,0:T(8,128)(2,1)} collective-permute-done((bf16[128,1024]{1,0:T(8,128)(2,1)}, bf16[128,1024]{1,0:T(8,128)(2,1)}, u32[]{:S(2)}, u32[]{:S(2)}) %collective-permute-start.11) | collective-permute-done | bytes 262176 | tf_op jit(solution)/shard_map/ppermute | solution.py:112
  258.4 4.9 %gather_fusion.1 = bf16[16,128,1024]{2,1,0:T(8,128)(2,1)} fusion(bf16[16,128,1024]{2,1,0:T(8,128)(2,1)} %bitcast_dynamic-update-slice_fusion, s32[1024]{0:T(1024)S(1)} %pad_clamp_fusion), kind=kCustom, calls=%fused_computation.1 | custom fusion | bytes 8388672 | tf_op jit(solution)/shard_map/gather | solution.py:117
  263.3 20.3 %collective-permute-start.19 = (bf16[2048,1024]{1,0:T(8,128)(2,1)}, bf16[2048,1024]{1,0:T(8,128)(2,1)}, u32[]{:S(2)}, u32[]{:S(2)}) collective-permute-start(bf16[2048,1024]{1,0:T(8,128)(2,1)} %bitcast.82), channel_id=1, source_target_pairs={{0,4},{4,0},{1,5},{5,1},{2,6},{6,2},{3,7},{7,3},{8,12},{12,8},{9,1... | collective-permute-start | bytes 12582920 | tf_op jit(solution)/shard_map/ppermute | solution.py:119
  283.6 7.1 %collective-permute-done.19 = bf16[2048,1024]{1,0:T(8,128)(2,1)} collective-permute-done((bf16[2048,1024]{1,0:T(8,128)(2,1)}, bf16[2048,1024]{1,0:T(8,128)(2,1)}, u32[]{:S(2)}, u32[]{:S(2)}) %collective-permute-start.19) | collective-permute-done | bytes 4194336 | tf_op jit(solution)/shard_map/ppermute | solution.py:119
  290.7 14.6 %fusion.30 = f32[2048,1024]{1,0:T(8,128)} fusion(bf16[2048,2048]{1,0:T(8,128)(2,1)} %all-gather.5.cloned.1.call-done, bf16[2048,1024]{1,0:T(8,128)(2,1)} %collective-permute-done.19), kind=kOutput, calls=%fused_computation.117 | convolution fusion | flops 8589934592 | bytes 20971520 | tf_op jit(solution)/shard_map/dot_general | solution.py:123
  305.3 16.0 %convolution_add_fusion = f32[2048,1024]{1,0:T(8,128)} fusion(f32[2048,1024]{1,0:T(8,128)} %fusion.30, bf16[2048,2048]{1,0:T(8,128)(2,1)} %all-gather.3.cloned.1.call-done, bf16[2048,1024]{1,0:T(8,128)(2,1)} %bitcast.83), kind=kOutput, calls=%fused_computation.5 | convolution fusion | flops 8592031744 | bytes 29360128 | tf_op jit(solution)/shard_map/dot_general | solution.py:121
  (113 shorter events, 86.8 us)
Async XLA Ops:
  7.2 283.5 %all-gather.5.cloned.1.call-start = ((), (), s32[]{:S(2)}) async-start(), calls=%async_computation.5 | async-start | bytes 8912896 | tf_op jit(solution)/shard_map/all_gather | solution.py:39
  8.7 3.0 collective-permute-start
  23.9 35.2 %all-to-all-start = ((bf16[16,48,1024]{2,1,0:T(8,128)(2,1)}), bf16[16,48,1024]{2,1,0:T(8,128)(2,1)}, u32[]{:S(2)}, u32[]{:S(2)}) async-start(bf16[16,48,1024]{2,1,0:T(8,128)(2,1)} %bitcast.81), calls=%async_computation | async-start | bytes 3145728 | tf_op jit(solution)/shard_map/all_to_all | solution.py:60
  64.5 19.8 %all-to-all-start.1 = ((f32[16,48,128]{2,1,0:T(8,128)}), f32[16,48,128]{2,1,0:T(8,128)S(1)}, u32[]{:S(2)}, u32[]{:S(2)}) async-start(f32[16,48,128]{2,1,0:T(8,128)} %bitcast.4), calls=%async_computation.1 | async-start | bytes 786432 | tf_op jit(solution)/shard_map/all_to_all | solution.py:69
  90.6 3.6 %collective-permute-start.2 = (f32[128,128]{0,1:T(8,128)S(1)}, f32[128,128]{0,1:T(8,128)S(1)}, u32[]{:S(2)}, u32[]{:S(2)}) collective-permute-start(f32[128,128]{0,1:T(8,128)S(1)} %copy.20), channel_id=1, source_target_pairs={{0,1},{1,0},{2,3},{3,2},{4,5},{5,4},{6,7},{7,6},{8,9},{9,8},{10,11... | collective-permute-start | bytes 196616 | tf_op jit(solution)/shard_map/ppermute | solution.py:78
  94.2 5.1 %collective-permute-start.3 = (f32[128,128]{0,1:T(8,128)S(1)}, f32[128,128]{0,1:T(8,128)S(1)}, u32[]{:S(2)}, u32[]{:S(2)}) collective-permute-start(f32[128,128]{0,1:T(8,128)S(1)} %add.181), channel_id=1, source_target_pairs={{0,2},{2,0},{1,3},{3,1},{4,6},{6,4},{5,7},{7,5},{8,10},{10,8},{9,1... | collective-permute-start | bytes 196616 | tf_op jit(solution)/shard_map/ppermute | solution.py:79
  106.9 10.7 %all-to-all-start.2 = ((bf16[16,48,128]{2,1,0:T(8,128)(2,1)}), bf16[16,48,128]{2,1,0:T(8,128)(2,1)S(1)}, u32[]{:S(2)}, u32[]{:S(2)}) async-start(bf16[16,48,128]{2,1,0:T(8,128)(2,1)} %bitcast.8), calls=%async_computation.2 | async-start | bytes 393216 | tf_op jit(solution)/shard_map/all_to_all | solution.py:91
  110.5 194.9 %all-gather.3.cloned.1.call-start = ((), (), s32[]{:S(2)}) async-start(), calls=%async_computation.4 | async-start | bytes 8912896 | tf_op jit(solution)/shard_map/all_gather | solution.py:38
  149.0 8.8 %collective-permute-start.4 = (bf16[128,1024]{1,0:T(8,128)(2,1)S(1)}, bf16[128,1024]{1,0:T(8,128)(2,1)S(1)}, u32[]{:S(2)}, u32[]{:S(2)}) collective-permute-start(bf16[128,1024]{1,0:T(8,128)(2,1)S(1)} %convolution_convert_fusion.2), channel_id=1, source_target_pairs={{0,8},{8,16},{16,24},{24,32},{32,40},{40,48},{48,56},{56,64},{64,7... | collective-permute-start | bytes 786440 | tf_op jit(solution)/shard_map/ppermute | solution.py:112
  157.7 10.5 %collective-permute-start.5 = (bf16[128,1024]{1,0:T(8,128)(2,1)S(1)}, bf16[128,1024]{1,0:T(8,128)(2,1)S(1)}, u32[]{:S(2)}, u32[]{:S(2)}) collective-permute-start(bf16[128,1024]{1,0:T(8,128)(2,1)S(1)} %collective-permute-done.4), channel_id=1, source_target_pairs={{0,8},{8,16},{16,24},{24,32},{32,40},{40,48},{48,56},{56,64},{64,7... | collective-permute-start | bytes 786440 | tf_op jit(solution)/shard_map/ppermute | solution.py:112
  157.7 13.8 %collective-permute-start.12 = (bf16[128,1024]{1,0:T(8,128)(2,1)S(1)}, bf16[128,1024]{1,0:T(8,128)(2,1)S(1)}, u32[]{:S(2)}, u32[]{:S(2)}) collective-permute-start(bf16[128,1024]{1,0:T(8,128)(2,1)S(1)} %convolution_convert_fusion.2), channel_id=1, source_target_pairs={{8,0},{16,8},{24,16},{32,24},{40,32},{48,40},{56,48},{64,56},{72,6... | collective-permute-start | bytes 786440 | tf_op jit(solution)/shard_map/ppermute | solution.py:114
  168.2 15.0 %collective-permute-start.6 = (bf16[128,1024]{1,0:T(8,128)(2,1)S(1)}, bf16[128,1024]{1,0:T(8,128)(2,1)S(1)}, u32[]{:S(2)}, u32[]{:S(2)}) collective-permute-start(bf16[128,1024]{1,0:T(8,128)(2,1)S(1)} %collective-permute-done.5), channel_id=1, source_target_pairs={{0,8},{8,16},{16,24},{24,32},{32,40},{40,48},{48,56},{56,64},{64,7... | collective-permute-start | bytes 786440 | tf_op jit(solution)/shard_map/ppermute | solution.py:112
  171.6 15.9 %collective-permute-start.13 = (bf16[128,1024]{1,0:T(8,128)(2,1)S(1)}, bf16[128,1024]{1,0:T(8,128)(2,1)S(1)}, u32[]{:S(2)}, u32[]{:S(2)}) collective-permute-start(bf16[128,1024]{1,0:T(8,128)(2,1)S(1)} %collective-permute-done.12), channel_id=1, source_target_pairs={{8,0},{16,8},{24,16},{32,24},{40,32},{48,40},{56,48},{64,56},{72,6... | collective-permute-start | bytes 786440 | tf_op jit(solution)/shard_map/ppermute | solution.py:114
  183.2 15.0 %collective-permute-start.7 = (bf16[128,1024]{1,0:T(8,128)(2,1)S(1)}, bf16[128,1024]{1,0:T(8,128)(2,1)S(1)}, u32[]{:S(2)}, u32[]{:S(2)}) collective-permute-start(bf16[128,1024]{1,0:T(8,128)(2,1)S(1)} %collective-permute-done.6), channel_id=1, source_target_pairs={{0,8},{8,16},{16,24},{24,32},{32,40},{40,48},{48,56},{56,64},{64,7... | collective-permute-start | bytes 786440 | tf_op jit(solution)/shard_map/ppermute | solution.py:112
  187.4 16.0 %collective-permute-start.14 = (bf16[128,1024]{1,0:T(8,128)(2,1)S(1)}, bf16[128,1024]{1,0:T(8,128)(2,1)S(1)}, u32[]{:S(2)}, u32[]{:S(2)}) collective-permute-start(bf16[128,1024]{1,0:T(8,128)(2,1)S(1)} %collective-permute-done.13), channel_id=1, source_target_pairs={{8,0},{16,8},{24,16},{32,24},{40,32},{48,40},{56,48},{64,56},{72,6... | collective-permute-start | bytes 786440 | tf_op jit(solution)/shard_map/ppermute | solution.py:114
  198.2 14.8 %collective-permute-start.8 = (bf16[128,1024]{1,0:T(8,128)(2,1)S(1)}, bf16[128,1024]{1,0:T(8,128)(2,1)S(1)}, u32[]{:S(2)}, u32[]{:S(2)}) collective-permute-start(bf16[128,1024]{1,0:T(8,128)(2,1)S(1)} %collective-permute-done.7), channel_id=1, source_target_pairs={{0,8},{8,16},{16,24},{24,32},{32,40},{40,48},{48,56},{56,64},{64,7... | collective-permute-start | bytes 786440 | tf_op jit(solution)/shard_map/ppermute | solution.py:112
  203.4 9.6 %collective-permute-start.15 = (bf16[128,1024]{1,0:T(8,128)(2,1)S(1)}, bf16[128,1024]{1,0:T(8,128)(2,1)S(1)}, u32[]{:S(2)}, u32[]{:S(2)}) collective-permute-start(bf16[128,1024]{1,0:T(8,128)(2,1)S(1)} %collective-permute-done.14), channel_id=1, source_target_pairs={{8,0},{16,8},{24,16},{32,24},{40,32},{48,40},{56,48},{64,56},{72,6... | collective-permute-start | bytes 786440 | tf_op jit(solution)/shard_map/ppermute | solution.py:114
  213.0 9.4 %collective-permute-start.9 = (bf16[128,1024]{1,0:T(8,128)(2,1)S(1)}, bf16[128,1024]{1,0:T(8,128)(2,1)S(1)}, u32[]{:S(2)}, u32[]{:S(2)}) collective-permute-start(bf16[128,1024]{1,0:T(8,128)(2,1)S(1)} %collective-permute-done.8), channel_id=1, source_target_pairs={{0,8},{8,16},{16,24},{24,32},{32,40},{40,48},{48,56},{56,64},{64,7... | collective-permute-start | bytes 786440 | tf_op jit(solution)/shard_map/ppermute | solution.py:112
  213.0 9.4 %collective-permute-start.16 = (bf16[128,1024]{1,0:T(8,128)(2,1)S(1)}, bf16[128,1024]{1,0:T(8,128)(2,1)S(1)}, u32[]{:S(2)}, u32[]{:S(2)}) collective-permute-start(bf16[128,1024]{1,0:T(8,128)(2,1)S(1)} %collective-permute-done.15), channel_id=1, source_target_pairs={{8,0},{16,8},{24,16},{32,24},{40,32},{48,40},{56,48},{64,56},{72,6... | collective-permute-start | bytes 786440 | tf_op jit(solution)/shard_map/ppermute | solution.py:114
  222.5 10.7 %collective-permute-start.10 = (bf16[128,1024]{1,0:T(8,128)(2,1)S(1)}, bf16[128,1024]{1,0:T(8,128)(2,1)}, u32[]{:S(2)}, u32[]{:S(2)}) collective-permute-start(bf16[128,1024]{1,0:T(8,128)(2,1)S(1)} %collective-permute-done.9), channel_id=1, source_target_pairs={{0,8},{8,16},{16,24},{24,32},{32,40},{40,48},{48,56},{56,64},{64,7... | collective-permute-start | bytes 786440 | tf_op jit(solution)/shard_map/ppermute | solution.py:112
  222.5 10.7 %collective-permute-start.17 = (bf16[128,1024]{1,0:T(8,128)(2,1)S(1)}, bf16[128,1024]{1,0:T(8,128)(2,1)S(1)}, u32[]{:S(2)}, u32[]{:S(2)}) collective-permute-start(bf16[128,1024]{1,0:T(8,128)(2,1)S(1)} %collective-permute-done.16), channel_id=1, source_target_pairs={{8,0},{16,8},{24,16},{32,24},{40,32},{48,40},{56,48},{64,56},{72,6... | collective-permute-start | bytes 786440 | tf_op jit(solution)/shard_map/ppermute | solution.py:114
  233.1 11.8 %collective-permute-start.11 = (bf16[128,1024]{1,0:T(8,128)(2,1)}, bf16[128,1024]{1,0:T(8,128)(2,1)}, u32[]{:S(2)}, u32[]{:S(2)}) collective-permute-start(bf16[128,1024]{1,0:T(8,128)(2,1)} %collective-permute-done.10), channel_id=1, source_target_pairs={{0,8},{8,16},{16,24},{24,32},{32,40},{40,48},{48,56},{56,64},{64,7... | collective-permute-start | bytes 786440 | tf_op jit(solution)/shard_map/ppermute | solution.py:112
  233.2 24.5 %collective-permute-start.18 = (bf16[128,1024]{1,0:T(8,128)(2,1)S(1)}, bf16[128,1024]{1,0:T(8,128)(2,1)S(1)}, u32[]{:S(2)}, u32[]{:S(2)}) collective-permute-start(bf16[128,1024]{1,0:T(8,128)(2,1)S(1)} %collective-permute-done.17), channel_id=1, source_target_pairs={{8,0},{16,8},{24,16},{32,24},{40,32},{48,40},{56,48},{64,56},{72,6... | collective-permute-start | bytes 786440 | tf_op jit(solution)/shard_map/ppermute | solution.py:114
  263.3 27.4 %collective-permute-start.19 = (bf16[2048,1024]{1,0:T(8,128)(2,1)}, bf16[2048,1024]{1,0:T(8,128)(2,1)}, u32[]{:S(2)}, u32[]{:S(2)}) collective-permute-start(bf16[2048,1024]{1,0:T(8,128)(2,1)} %bitcast.82), channel_id=1, source_target_pairs={{0,4},{4,0},{1,5},{5,1},{2,6},{6,2},{3,7},{7,3},{8,12},{12,8},{9,1... | collective-permute-start | bytes 12582920 | tf_op jit(solution)/shard_map/ppermute | solution.py:119
  (8 other events, 112.2 us)
Sparse Core Ops, SparseCore 0:
  12.7 91.3 all-gather.4
  113.4 105.6 all-gather.2
